TPU v7x, 32 devices: a whole 2x2x4 slice. The times are simulated.
32 devices in a mesh: groups: 2 (over x), ctx: 16 (over z, y, core).
Axes of the slice: x: 2, y: 2, z: 4, core: 2. Of those that a mesh axis runs over, the one named last changes fastest.
Arguments:
- query: bfloat16 [8192, 1024], P(('groups', 'ctx')), parts along dimension 0, may hold values from -130 to 130, as said below
- key: bfloat16 [8192, 1024], P(('groups', 'ctx')), parts along dimension 0, may hold values from -4.5 to 4.5
- value: bfloat16 [8192, 1024], P(('groups', 'ctx')), parts along dimension 0, may hold values from -6 to 6
- cotangent: bfloat16 [8192, 1024], P(('groups', 'ctx')), parts along dimension 0, may hold values from -6 to 6
- global_ids: int32 [4], P('groups'), parts along dimension 0, may hold values from 0 to 63
- rand_owner: int32 [128, 6], P('groups'), parts along dimension 0, may hold values from 0 to 15, all different within a row; in each aligned block of 4 rows (0 to 3, 4 to 7, ...) at most 2 rows name the same one
- rand_local: int32 [128, 6], P('groups'), parts along dimension 0, may hold values from 0 to 3
Outputs:
- attended: bfloat16 [8192, 1024], P(('groups', 'ctx')), parts along dimension 0
- grad_query: bfloat16 [8192, 1024], P(('groups', 'ctx')), parts along dimension 0
- grad_key: bfloat16 [8192, 1024], P(('groups', 'ctx')), parts along dimension 0
- grad_value: bfloat16 [8192, 1024], P(('groups', 'ctx')), parts along dimension 0
There are 2 independent parts, one for each index of `groups`. A program takes and returns all parts, laid end to end along the dimension named above; each array names one. Nothing has to cross between parts.
Inputs may be any that keep to these rules, and one draw needn't show every extreme that they name: query and key are drawn together. `rand_owner`: each row names 6 different devices. In the 4 rows of one device no device is named more than 2 times, and in some device's rows some device is named exactly 2 times.
All inputs are finite; a program needn't handle non-finite values.
Results may differ from a plain program's by a relative error of at most 0.017.
Values may be sent and summed in bfloat16 or wider, within the bound.
A program may use at most 192 MiB of HBM per device.

v0:
```python
import jax
import jax.numpy as jnp
from jax import lax
from jax.sharding import PartitionSpec as P

HEAD_DIM = 64
GROUP_HEADS = 8
BLOCK = 64
GLOBALS = 2
ROUNDS = 3
NEG_FILL = -1e30


def padded_2(block, sides, width):
    for axis, dim in sides:
        count = lax.axis_size(axis)
        forward = [(i, i + 1) for i in range(count - 1)]
        backward = [(target, source) for source, target in forward]
        low = lax.ppermute(
            lax.slice_in_dim(block, block.shape[dim] - width, None, axis=dim), axis, forward
        )
        high = lax.ppermute(lax.slice_in_dim(block, 0, width, axis=dim), axis, backward)
        block = jnp.concatenate([low, block, high], axis=dim)
    return block


def broadcast(array, axis, root):
    mine = lax.axis_index(axis) == root
    return lax.psum(jnp.where(mine, array, jnp.zeros_like(array)), axis)


def request_ranks(owners, device_count):
    onehot = (owners[:, :, None] == jnp.arange(device_count, dtype=jnp.int32)).astype(jnp.int32)
    before = jnp.cumsum(onehot, axis=1) - onehot
    return jnp.sum(before * onehot, axis=2)


def per_device(query, key, value, cotangent, global_ids, rand_owner, rand_local):
    tok_count, features = query.shape
    blocks = tok_count // BLOCK
    head_count = features // HEAD_DIM
    groups = head_count // GROUP_HEADS
    group_width = GROUP_HEADS * HEAD_DIM
    device_count = lax.axis_size("ctx")
    my_index = lax.axis_index("ctx")
    pick_count = groups * ROUNDS
    slot_count = max(2, (pick_count * blocks + device_count - 1) // device_count)
    score_scale = HEAD_DIM ** (-0.5)
    key_kinds = 3 + GLOBALS + ROUNDS
    key_span = key_kinds * BLOCK
    kv_local = jnp.stack(
        (key.reshape(blocks, BLOCK, features), value.reshape(blocks, BLOCK, features)), axis=2
    )
    padded = padded_2(kv_local, (("ctx", 0),), 1)
    glob_list = []
    for glob_index in range(GLOBALS):
        root_dev = global_ids[glob_index] // blocks
        local_block = global_ids[glob_index] % blocks
        block_kv = lax.dynamic_index_in_dim(kv_local, local_block, 0, keepdims=False)
        glob_list.append(broadcast(block_kv, "ctx", root_dev))
    glob_kv = jnp.stack(glob_list)
    owners_all = rand_owner.reshape(device_count, blocks * pick_count)
    locals_all = rand_local.reshape(device_count, blocks * pick_count)
    ranks_all = request_ranks(owners_all, device_count)
    my_owner = lax.dynamic_index_in_dim(owners_all, my_index, 0, keepdims=False)
    my_rank = lax.dynamic_index_in_dim(ranks_all, my_index, 0, keepdims=False)
    fetch_index = my_owner * slot_count + my_rank
    entry_group = jnp.arange(blocks * pick_count, dtype=jnp.int32) % pick_count // ROUNDS
    matched = (
        (owners_all[:, :, None] == my_index)
        & (ranks_all[:, :, None] == jnp.arange(slot_count, dtype=jnp.int32))
    ).astype(jnp.int32)
    send_block = jnp.sum(matched * locals_all[:, :, None], axis=1).reshape(-1)
    send_group = jnp.sum(matched * entry_group[None, :, None], axis=1).reshape(-1)
    send_live = jnp.sum(matched, axis=1).reshape(-1) > 0
    kv_grouped = kv_local.reshape(blocks, BLOCK, 2, groups, group_width)

    def pack_blocks():
        picked = kv_grouped[send_block, :, :, send_group, :]
        picked = jnp.where(send_live[:, None, None, None], picked, jnp.zeros((), picked.dtype))
        return picked.reshape(device_count, slot_count, BLOCK, 2, group_width)

    def unpack_blocks(arrived):
        arrived_flat = arrived.reshape(device_count * slot_count, BLOCK, 2, group_width)
        return arrived_flat[fetch_index].reshape(blocks, groups, ROUNDS, BLOCK, 2, group_width)

    random_kv = unpack_blocks(
        lax.all_to_all(pack_blocks(), "ctx", split_axis=0, concat_axis=0, tiled=True)
    )
    block_ids = jnp.arange(blocks)
    left_ok = jnp.logical_or(my_index > 0, block_ids > 0)
    right_ok = jnp.logical_or(my_index < device_count - 1, block_ids < blocks - 1)
    key_valid = jnp.concatenate(
        (
            jnp.repeat(left_ok[:, None], BLOCK, axis=1),
            jnp.ones((blocks, BLOCK), jnp.bool_),
            jnp.repeat(right_ok[:, None], BLOCK, axis=1),
            jnp.ones((blocks, (GLOBALS + ROUNDS) * BLOCK), jnp.bool_),
        ),
        axis=1,
    )
    valid_four = key_valid[:, None, None, :]

    def assemble(group_idx, source_kv):
        start_col = group_idx * group_width
        window = jnp.stack(
            [
                padded[offset : offset + blocks, :, :, start_col : start_col + group_width]
                for offset in range(3)
            ],
            axis=1,
        )
        global_part = jnp.broadcast_to(
            glob_kv[None, :, :, :, start_col : start_col + group_width],
            (blocks, GLOBALS, BLOCK, 2, group_width),
        )
        random_part = source_kv[:, group_idx]
        joined = jnp.concatenate((window, global_part, random_part), axis=1)
        joined = joined.reshape(blocks, key_span, 2, GROUP_HEADS, HEAD_DIM)
        return (joined[:, :, 0], joined[:, :, 1])

    def score_block(query_group, keys_group):
        scores = (
            jnp.einsum(
                "bqhd,bkhd->bhqk", query_group, keys_group, preferred_element_type=jnp.float32
            )
            * score_scale
        )
        return jnp.where(valid_four, scores, NEG_FILL)

    query_blocks = query.reshape(blocks, BLOCK, groups, GROUP_HEADS, HEAD_DIM)
    cot_blocks = cotangent.reshape(blocks, BLOCK, groups, GROUP_HEADS, HEAD_DIM)
    attended_parts = []
    totals = []
    for group_idx in range(groups):
        keys_group, vals_group = assemble(group_idx, random_kv)
        scores = score_block(query_blocks[:, :, group_idx], keys_group)
        row_max = jnp.max(scores, axis=-1, keepdims=True)
        weights = jnp.where(valid_four, jnp.exp(scores - row_max), 0.0)
        log_total = row_max + jnp.log(jnp.sum(weights, axis=-1, keepdims=True))
        probs_b = jnp.where(valid_four, jnp.exp(scores - log_total), 0.0).astype(jnp.bfloat16)
        attended_parts.append(
            jnp.einsum(
                "bhqk,bkhd->bqhd", probs_b, vals_group, preferred_element_type=jnp.float32
            ).astype(jnp.bfloat16)
        )
        totals.append(log_total)
    back_kv = unpack_blocks(
        lax.all_to_all(pack_blocks(), "ctx", split_axis=0, concat_axis=0, tiled=True)
    )
    win_acc = jnp.zeros((blocks + 2, BLOCK, 2, features), jnp.float32)
    glob_acc = jnp.zeros((GLOBALS, BLOCK, 2, features), jnp.float32)
    grad_query_parts = []
    random_terms = []
    for group_idx in range(groups):
        start_col = group_idx * group_width
        keys_group, vals_group = assemble(group_idx, back_kv)
        query_group = query_blocks[:, :, group_idx]
        cot_group = cot_blocks[:, :, group_idx]
        scores = score_block(query_group, keys_group)
        probs = jnp.where(valid_four, jnp.exp(scores - totals[group_idx]), 0.0)
        probs_b = probs.astype(jnp.bfloat16)
        row_dot = jnp.sum(
            cot_group.astype(jnp.float32) * attended_parts[group_idx].astype(jnp.float32), axis=-1
        )
        row_dot = jnp.transpose(row_dot, (0, 2, 1))[..., None]
        dprob = jnp.einsum(
            "bqhd,bkhd->bhqk", cot_group, vals_group, preferred_element_type=jnp.float32
        )
        dscore = (probs * (dprob - row_dot)).astype(jnp.bfloat16)
        grad_query_parts.append(
            (
                jnp.einsum(
                    "bhqk,bkhd->bqhd", dscore, keys_group, preferred_element_type=jnp.float32
                )
                * score_scale
            ).astype(jnp.bfloat16)
        )
        term_k = (
            jnp.einsum("bhqk,bqhd->bkhd", dscore, query_group, preferred_element_type=jnp.float32)
            * score_scale
        )
        term_v = jnp.einsum(
            "bhqk,bqhd->bkhd", probs_b, cot_group, preferred_element_type=jnp.float32
        )
        term_kv = jnp.stack((term_k, term_v), axis=2).reshape(
            blocks, key_kinds, BLOCK, 2, group_width
        )
        for offset in range(3):
            win_acc = win_acc.at[
                offset : offset + blocks, :, :, start_col : start_col + group_width
            ].add(term_kv[:, offset])
        glob_acc = glob_acc.at[:, :, :, start_col : start_col + group_width].add(
            jnp.sum(term_kv[:, 3 : 3 + GLOBALS], axis=0)
        )
        random_terms.append(term_kv[:, 3 + GLOBALS :].astype(jnp.bfloat16))
    random_flat = jnp.stack(random_terms, axis=1).reshape(
        blocks * pick_count, BLOCK, 2, group_width
    )
    grad_send = (
        jnp.zeros((device_count * slot_count, BLOCK, 2, group_width), jnp.bfloat16)
        .at[fetch_index]
        .set(random_flat)
    )
    grad_back = lax.all_to_all(
        grad_send.reshape(device_count, slot_count, BLOCK, 2, group_width),
        "ctx",
        split_axis=0,
        concat_axis=0,
        tiled=True,
    )
    grad_back = grad_back.reshape(device_count * slot_count, BLOCK, 2, group_width).astype(
        jnp.float32
    )
    grad_back = jnp.where(send_live[:, None, None, None], grad_back, 0.0)
    grad_owned = jnp.zeros((blocks, BLOCK, 2, groups, group_width), jnp.float32)
    grad_owned = grad_owned.at[send_block, :, :, send_group, :].add(grad_back)
    edge_sums = jnp.stack((win_acc[0], win_acc[blocks + 1]))
    edge_ext = padded_2(edge_sums, (("ctx", 0),), 1)
    glob_summed = lax.psum(glob_acc, "ctx")
    grad_total = win_acc[1 : blocks + 1] + grad_owned.reshape(blocks, BLOCK, 2, features)
    grad_total = grad_total.at[0].add(edge_ext[0]).at[blocks - 1].add(edge_ext[3])
    first_id = my_index * blocks + jnp.arange(blocks)
    for glob_index in range(GLOBALS):
        is_owner = global_ids[glob_index] == first_id
        grad_total = grad_total + jnp.where(
            is_owner[:, None, None, None], glob_summed[glob_index][None], 0.0
        )
    attended = jnp.stack(attended_parts, axis=2).reshape(tok_count, features)
    grad_query = jnp.stack(grad_query_parts, axis=2).reshape(tok_count, features)
    grad_key = grad_total[:, :, 0].reshape(tok_count, features).astype(jnp.bfloat16)
    grad_value = grad_total[:, :, 1].reshape(tok_count, features).astype(jnp.bfloat16)
    return (attended, grad_query, grad_key, grad_value)


def solution(mesh):
    return jax.shard_map(
        per_device,
        mesh=mesh,
        in_specs=(
            P(("groups", "ctx"), None),
            P(("groups", "ctx"), None),
            P(("groups", "ctx"), None),
            P(("groups", "ctx"), None),
            P("groups"),
            P("groups", None),
            P("groups", None),
        ),
        out_specs=(
            P(("groups", "ctx"), None),
            P(("groups", "ctx"), None),
            P(("groups", "ctx"), None),
            P(("groups", "ctx"), None),
        ),
        check_vma=False,
    )
```

profile of v0, /device:TPU:0, one launch (start us, length us, event | category | flops | bytes accessed | tf_op | source)
XLA Modules:
  0.0 544.2 jit_solution(3733437625669096891)
XLA Ops:
  12.2 2.8 gather_fusion
  15.0 4.5 broadcast_select_fusion
  19.4 7.6 %all-to-all-start = ((bf16[16,2,64,2,512]{4,2,3,1,0:T(8,128)(2,1)}), bf16[16,2,64,2,512]{4,2,3,1,0:T(8,128)(2,1)}, u32[]{:S(2)}, u32[]{:S(2)}) async-start(bf16[16,2,64,2,512]{4,2,3,1,0:T(8,128)(2,1)} %broadcast_select_fusion), calls=%async_computation | async-start | bytes 8388608 | tf_op jit(solution)/shard_map/all_to_all | solution.py:88
  33.9 3.0 collective-permute-start
  43.8 2.1 copy.242
  45.9 2.1 copy.241
  48.0 2.0 fusion.71
  50.0 130.4 %all-reduce.7.cloned.1.call-done = (bf16[1,64,2,1024]{3,1,2,0:T(8,128)(2,1)}, bf16[1,64,2,1024]{3,1,2,0:T(8,128)(2,1)}) async-done(((bf16[1,64,2,1024]{3,1,2,0:T(8,128)(2,1)}, bf16[1,64,2,1024]{3,1,2,0:T(8,128)(2,1)}), (bf16[1,64,2,1024]{3,1,2,0:T(8,128)(2,1)}, bf16[1,64,2,1024]{3,1,2,0:T(8,128)(2,1)})) %all-reduce.7.cloned.1.call-update) | async-done | bytes 524304 | tf_op jit(solution)/shard_map/psum | solution.py:29
  183.4 2.0 fusion.70
  187.1 2.9 gather_fusion.1
  191.9 10.0 %copy.236 = bf16[4,8,64,2,512]{2,1,4,0,3:T(8,128)(2,1)} copy(bf16[4,8,64,2,512]{4,2,3,1,0:T(8,128)(2,1)} %get-tuple-element.138) | data formatting | bytes 8388608 | tf_op jit(solution)/shard_map/reshape | solution.py:119
  201.9 11.8 %reshape.691 = bf16[4,512,2,8,64]{1,4,3,0,2:T(8,128)(2,1)} reshape(bf16[4,8,64,2,512]{2,1,4,0,3:T(8,128)(2,1)} %copy.236) | data formatting | bytes 8388608 | tf_op jit(solution)/shard_map/reshape | solution.py:119
  213.7 10.0 %copy.234 = bf16[4,8,64,2,512]{2,1,4,0,3:T(8,128)(2,1)} copy(bf16[4,8,64,2,512]{4,2,3,1,0:T(8,128)(2,1)} %get-tuple-element.137) | data formatting | bytes 8388608 | tf_op jit(solution)/shard_map/reshape | solution.py:119
  223.8 11.8 %reshape.690 = bf16[4,512,2,8,64]{1,4,3,0,2:T(8,128)(2,1)} reshape(bf16[4,8,64,2,512]{2,1,4,0,3:T(8,128)(2,1)} %copy.234) | data formatting | bytes 8388608 | tf_op jit(solution)/shard_map/reshape | solution.py:119
  235.6 2.4 fusion.25
  240.0 2.3 fusion.9
  242.3 2.2 multiply_reduce_fusion
  244.6 3.2 convolution_bitcast_fusion
  247.8 2.2 multiply_reduce_fusion.1
  250.0 3.2 convolution_bitcast_fusion.1
  253.2 2.2 fusion
  255.5 2.6 fusion.1
  258.1 7.1 %reshape.688 = f32[4,8,64,1,512]{2,1,4,0,3:T(8,128)} reshape(f32[4,512,8,64]{1,3,2,0:T(8,128)} %convolution_bitcast_fusion) | data formatting | bytes 8388608 | tf_op jit(solution)/shard_map/stack | solution.py:186
  265.2 6.8 %copy.232 = f32[4,8,64,1,512]{4,2,1,0,3:T(8,128)} copy(f32[4,8,64,1,512]{2,1,4,0,3:T(8,128)} %reshape.688) | data formatting | bytes 8388608 | tf_op jit(solution)/shard_map/stack | solution.py:186
  272.0 2.7 multiply_bitcast_fusion
  274.7 7.1 %reshape.687 = f32[4,8,64,1,512]{2,1,4,0,3:T(8,128)} reshape(f32[4,512,8,64]{1,3,2,0:T(8,128)} %multiply_bitcast_fusion) | data formatting | bytes 8388608 | tf_op jit(solution)/shard_map/stack | solution.py:186
  281.8 6.8 %copy.231 = f32[4,8,64,1,512]{4,2,1,0,3:T(8,128)} copy(f32[4,8,64,1,512]{2,1,4,0,3:T(8,128)} %reshape.687) | data formatting | bytes 8388608 | tf_op jit(solution)/shard_map/stack | solution.py:186
  288.6 7.1 %reshape.686 = f32[4,8,64,1,512]{2,1,4,0,3:T(8,128)} reshape(f32[4,512,8,64]{1,3,2,0:T(8,128)} %convolution_bitcast_fusion.1) | data formatting | bytes 8388608 | tf_op jit(solution)/shard_map/stack | solution.py:186
  295.6 7.0 %copy.230 = f32[4,8,64,1,512]{4,2,1,0,3:T(8,128)} copy(f32[4,8,64,1,512]{2,1,4,0,3:T(8,128)} %reshape.686) | data formatting | bytes 8388608 | tf_op jit(solution)/shard_map/stack | solution.py:186
  302.6 2.7 multiply_bitcast_fusion.1
  305.3 7.1 %reshape.685 = f32[4,8,64,1,512]{2,1,4,0,3:T(8,128)} reshape(f32[4,512,8,64]{1,3,2,0:T(8,128)} %multiply_bitcast_fusion.1) | data formatting | bytes 8388608 | tf_op jit(solution)/shard_map/stack | solution.py:186
  312.4 6.9 %copy.229 = f32[4,8,64,1,512]{4,2,1,0,3:T(8,128)} copy(f32[4,8,64,1,512]{2,1,4,0,3:T(8,128)} %reshape.685) | data formatting | bytes 8388608 | tf_op jit(solution)/shard_map/stack | solution.py:186
  319.3 2.3 fusion.27
  324.5 2.5 broadcast_in_dim.190
  326.9 7.5 %scatter_fusion = bf16[32,64,2,512]{3,1,2,0:T(8,128)(2,1)} fusion(bf16[32,64,2,512]{3,1,2,0:T(8,128)(2,1)} %broadcast_in_dim.190, s32[24]{0:T(128)S(1)} %fusion.86, bf16[24,64,2,512]{3,1,2,0:T(8,128)(2,1)S(1)} %bitcast.294), kind=kCustom, calls=%fused_computation.2 | custom fusion | bytes 9437280 | tf_op jit(solution)/shard_map/scatter | solution.py:203
  334.5 5.4 all-to-all-start.1
  346.8 3.1 fusion.36
  350.2 2.3 fusion.37
  363.1 3.1 add_select_fusion
  366.2 5.7 %scatter-add.41 = f32[6,64,2,1024]{3,1,0,2:T(8,128)S(1)} dynamic-update-slice(f32[6,64,2,1024]{3,1,0,2:T(8,128)S(1)} %fusion.58, f32[4,64,2,512]{3,1,0,2:T(8,128)} %add_select_fusion, s32[]{:T(128)} %bitcast.48, s32[]{:T(128)} %constant.374.clone.1, s32[]{:T(128)} %constant.374.clone.1, s32[]{:T(128)} %bitcast.49) | dynamic-update-slice | bytes 2097156 | tf_op jit(solution)/shard_map/scatter-add | solution.py:192
  382.5 3.1 collective-permute-start.2
  386.9 115.4 %all-reduce.5.cloned.1.call-done = f32[2,64,2,1024]{3,1,0,2:T(8,128)} async-done(((f32[2,64,2,1024]{3,1,0,2:T(8,128)}), f32[2,64,2,1024]{3,1,0,2:T(8,128)}) %all-reduce.5.cloned.1.call-update) | async-done | bytes 1048592 | tf_op jit(solution)/shard_map/psum | solution.py:220
  502.3 2.3 slice_bitcast_fusion.31
  504.6 6.9 %convert_select_fusion = f32[32,64,2,512]{3,1,2,0:T(8,128)} fusion(bf16[16,2,64,2,512]{4,2,3,1,0:T(8,128)(2,1)} %all-to-all-done.1, pred[32]{0:T(512)(128)(4,1)S(1)} %gt.20), kind=kLoop, calls=%fused_computation.20 | loop fusion | flops 4194304 | bytes 12582944 | tf_op jit(solution)/shard_map/jit(_where)/select_n | solution.py:215
  511.7 12.3 %scatter_fusion.1 = f32[4,64,2,2,512]{4,1,3,2,0:T(8,128)S(1)} fusion(f32[4,64,2,2,512]{4,1,3,2,0:T(8,128)S(1)} %broadcast_in_dim.188, s32[32]{0:T(128)S(1)} %get-tuple-element.133, f32[32,64,2,512]{3,1,2,0:T(8,128)} %convert_select_fusion), kind=kCustom, calls=%fused_computation.3 | custom fusion | flops 2097152 | bytes 25166080 | tf_op jit(solution)/shard_map/scatter-add | solution.py:217
  524.0 2.9 copy.233
  527.0 4.2 reshape.689
  531.2 2.1 slice_add_fusion
  (154 shorter events, 58.4 us)
Async XLA Ops:
  7.2 3.1 copy-start.28
  7.2 4.0 copy-start.29
  19.4 7.7 %copy-start.30 = (s32[2]{0:T(128)S(1)}, s32[2]{0:T(128)}, u32[]{:S(2)}) copy-start(s32[2]{0:T(128)} %param.31) | copy-start | bytes 28
  19.4 13.5 %copy-start.12 = (bf16[256,1024]{1,0:T(8,128)(2,1)S(1)}, bf16[256,1024]{1,0:T(8,128)(2,1)}, u32[]{:S(2)}) copy-start(bf16[256,1024]{1,0:T(8,128)(2,1)} %param.28) | copy-start | bytes 1572868
  19.4 13.5 %copy-start.13 = (bf16[256,1024]{1,0:T(8,128)(2,1)S(1)}, bf16[256,1024]{1,0:T(8,128)(2,1)}, u32[]{:S(2)}) copy-start(bf16[256,1024]{1,0:T(8,128)(2,1)} %param.29) | copy-start | bytes 1572868
  19.4 19.0 %copy-start.25 = (bf16[256,1024]{1,0:T(8,128)(2,1)S(1)}, bf16[256,1024]{1,0:T(8,128)(2,1)}, u32[]{:S(2)}) copy-start(bf16[256,1024]{1,0:T(8,128)(2,1)} %param.30) | copy-start | bytes 1572868
  19.4 167.6 %all-to-all-start = ((bf16[16,2,64,2,512]{4,2,3,1,0:T(8,128)(2,1)}), bf16[16,2,64,2,512]{4,2,3,1,0:T(8,128)(2,1)}, u32[]{:S(2)}, u32[]{:S(2)}) async-start(bf16[16,2,64,2,512]{4,2,3,1,0:T(8,128)(2,1)} %broadcast_select_fusion), calls=%async_computation | async-start | bytes 8388608 | tf_op jit(solution)/shard_map/all_to_all | solution.py:88
  27.1 153.4 %all-reduce.7.cloned.1.call-start = ((), (), s32[]{:S(2)}) async-start(), calls=%async_computation.3 | async-start | bytes 1048576 | tf_op jit(solution)/shard_map/psum | solution.py:29
  33.9 14.1 %collective-permute-start = (bf16[1,64,2,1024]{3,1,2,0:T(8,128)(2,1)}, bf16[1,64,2,1024]{3,1,2,0:T(8,128)(2,1)}, u32[]{:S(2)}, u32[]{:S(2)}) collective-permute-start(bf16[1,64,2,1024]{3,1,2,0:T(8,128)(2,1)} %get-tuple-element.154), channel_id=1, source_target_pairs={{0,1},{1,2},{2,3},{3,4},{4,5},{5,6},{6,7},{7,8},{8,9},{9,10},{10,1... | collective-permute-start | bytes 786440 | tf_op jit(solution)/shard_map/ppermute | solution.py:19
  36.9 146.6 %collective-permute-start.1 = (bf16[1,64,2,1024]{3,1,2,0:T(8,128)(2,1)S(1)}, bf16[1,64,2,1024]{3,1,2,0:T(8,128)(2,1)}, u32[]{:S(2)}, u32[]{:S(2)}) collective-permute-start(bf16[1,64,2,1024]{3,1,2,0:T(8,128)(2,1)S(1)} %get-tuple-element.155), channel_id=1, source_target_pairs={{1,0},{2,1},{3,2},{4,3},{5,4},{6,5},{7,6},{8,7},{9,8},{10,9},{11,1... | collective-permute-start | bytes 786440 | tf_op jit(solution)/shard_map/ppermute | solution.py:22
  223.7 11.8 %copy-start.18 = (bf16[4,64,1,8,64]{4,3,2,1,0:T(8,128)(2,1)S(1)}, bf16[4,64,1,8,64]{4,3,2,1,0:T(8,128)(2,1)}, u32[]{:S(2)}) copy-start(bf16[4,64,1,8,64]{4,3,2,1,0:T(8,128)(2,1)} %get-tuple-element.150) | copy-start | bytes 786436
  235.6 2.8 copy-start.15
  235.6 2.9 copy-start.17
  239.9 2.4 copy-start.14
  240.0 2.4 copy-start.20
  244.6 3.2 copy-start.19
  255.5 16.5 %copy-start.21 = (bf16[4,8,64,512]{3,2,1,0:T(8,128)(2,1)}, bf16[4,8,64,512]{3,2,1,0:T(8,128)(2,1)S(1)}, u32[]{:S(2)}) copy-start(bf16[4,8,64,512]{3,2,1,0:T(8,128)(2,1)S(1)} %fusion) | copy-start | bytes 6291460
  295.6 7.0 %copy-start.22 = (bf16[4,8,64,512]{3,2,1,0:T(8,128)(2,1)S(1)}, bf16[4,8,64,512]{3,2,1,0:T(8,128)(2,1)}, u32[]{:S(2)}) copy-start(bf16[4,8,64,512]{3,2,1,0:T(8,128)(2,1)} %fusion.1) | copy-start | bytes 6291460
  319.3 3.1 copy-start.4
  319.3 4.4 copy-start.7
  334.5 7.5 %copy-start.31 = (s32[4]{0:T(128)S(1)}, s32[4]{0:T(128)}, u32[]{:S(2)}) copy-start(s32[4]{0:T(128)} %constant.391.clone.1) | copy-start | bytes 52
  334.5 9.4 %copy-start.26 = (bf16[4,8,64,64]{3,2,1,0:T(8,128)(2,1)S(1)}, bf16[4,8,64,64]{3,2,1,0:T(8,128)(2,1)}, u32[]{:S(2)}) copy-start(bf16[4,8,64,64]{3,2,1,0:T(8,128)(2,1)} %get-tuple-element.165) | copy-start | bytes 786436
  334.5 9.4 %copy-start.27 = (bf16[4,8,64,64]{3,2,1,0:T(8,128)(2,1)S(1)}, bf16[4,8,64,64]{3,2,1,0:T(8,128)(2,1)}, u32[]{:S(2)}) copy-start(bf16[4,8,64,64]{3,2,1,0:T(8,128)(2,1)} %get-tuple-element.167) | copy-start | bytes 786436
  334.5 170.1 %all-to-all-start.1 = ((bf16[16,2,64,2,512]{4,2,3,1,0:T(8,128)(2,1)}), bf16[16,2,64,2,512]{4,2,3,1,0:T(8,128)(2,1)}, u32[]{:S(2)}, u32[]{:S(2)}) async-start(bf16[16,2,64,2,512]{4,2,3,1,0:T(8,128)(2,1)} %bitcast.283), calls=%async_computation.1 | async-start | bytes 8388608 | tf_op jit(solution)/shard_map/all_to_all | solution.py:205
  339.8 162.5 %all-reduce.5.cloned.1.call-start = ((), (), s32[]{:S(2)}) async-start(), calls=%async_computation.2 | async-start | bytes 2097152 | tf_op jit(solution)/shard_map/psum | solution.py:220
  346.8 3.4 copy-start.16
  355.3 2.5 copy-start.8
  356.8 2.6 copy-start.5
  359.6 2.2 copy-start
  359.6 3.5 copy-start.2
  371.9 2.8 copy-start.6
  371.9 4.1 copy-start.9
  377.3 2.5 copy-start.1
  377.3 3.8 copy-start.3
  381.4 130.1 %copy-start.10 = (f32[6,64,2,1024]{3,1,0,2:T(8,128)}, f32[6,64,2,1024]{3,1,0,2:T(8,128)S(1)}, u32[]{:S(2)}) copy-start(f32[6,64,2,1024]{3,1,0,2:T(8,128)S(1)} %fusion.48) | copy-start | bytes 9437188
  382.5 150.7 %collective-permute-start.2 = (f32[1,64,2,1024]{3,1,0,2:T(8,128)}, f32[1,64,2,1024]{3,1,0,2:T(8,128)}, u32[]{:S(2)}, u32[]{:S(2)}) collective-permute-start(f32[1,64,2,1024]{3,1,0,2:T(8,128)} %get-tuple-element.136), channel_id=1, source_target_pairs={{0,1},{1,2},{2,3},{3,4},{4,5},{5,6},{6,7},{7,8},{8,9},{9,10},{10,1... | collective-permute-start | bytes 1572872 | tf_op jit(solution)/shard_map/ppermute | solution.py:19
  385.6 148.8 %collective-permute-start.3 = (f32[1,64,2,1024]{3,1,0,2:T(8,128)}, f32[1,64,2,1024]{3,1,0,2:T(8,128)}, u32[]{:S(2)}, u32[]{:S(2)}) collective-permute-start(f32[1,64,2,1024]{3,1,0,2:T(8,128)} %get-tuple-element.135), channel_id=1, source_target_pairs={{1,0},{2,1},{3,2},{4,3},{5,4},{6,5},{7,6},{8,7},{9,8},{10,9},{11,1... | collective-permute-start | bytes 1572872 | tf_op jit(solution)/shard_map/ppermute | solution.py:22
  527.0 4.2 copy-start.11
  531.1 4.5 copy-start.23
  531.1 4.5 copy-start.24
Sparse Core Ops, SparseCore 0:
  38.6 141.7 all-reduce.6
  377.4 124.8 all-reduce.4
where the time goes:
time: 550 us; the launch traced here: 544 us
  waiting for transfers between devices  246 us (45%)
  local copies, waits for them, and re-layouts  171 us (31%)
  other arithmetic  55 us (10%)
  matrix products  30.4 us (6%)
  starting transfers between devices  22 us (4%)
  between operations  20.1 us (4%)
    psum x1, waiting for transfers between devices, broadcast(): return lax.psum(jnp.where(mine, array, jnp.zeros_like(array)), axis)  130 us
    psum x1, waiting for transfers between devices, per_device(): glob_summed = lax.psum(glob_acc, 'ctx')  115 us
    another operation x8, local copies, waits for them, and re-layouts, per_device(): jnp.stack((term_k, term_v), axis=2)  55.7 us
    reshape x4, local copies, waits for them, and re-layouts, assemble(): joined = joined.reshape(blocks, key_span, 2, GROUP_HEADS, HEAD_DIM)  43.7 us
    unnamed x70, local copies, waits for them, and re-layouts  19.5 us
    scatter-add x1, other arithmetic, per_device(): grad_owned = grad_owned.at[send_block, :, :, send_group, :].add(grad_back)  12.3 us
  transfers between devices with their start and end apart: 8, of which 2 were waited for; matrix products, arithmetic and copies ran while one was open for 15% of the time, Pallas kernels for 0%

commit v1 on v0

--- a/solution.py
+++ b/solution.py
@@ -217,7 +217,8 @@
     grad_owned = grad_owned.at[send_block, :, :, send_group, :].add(grad_back)
     edge_sums = jnp.stack((win_acc[0], win_acc[blocks + 1]))
     edge_ext = padded_2(edge_sums, (("ctx", 0),), 1)
-    glob_summed = lax.psum(glob_acc, "ctx")
+    main = jax.lax.all_gather(glob_acc, "ctx")
+    glob_summed = jnp.sum(main, 0)
     grad_total = win_acc[1 : blocks + 1] + grad_owned.reshape(blocks, BLOCK, 2, features)
     grad_total = grad_total.at[0].add(edge_ext[0]).at[blocks - 1].add(edge_ext[3])
     first_id = my_index * blocks + jnp.arange(blocks)

time: 550 us -> 585 us (1.064)
  the two profiles are of different devices: /device:TPU:0 before, /device:TPU:15 now
where the time goes in v1:
time: 585 us; the launch traced here: 579 us
  waiting for transfers between devices  267 us (46%)
  local copies, waits for them, and re-layouts  170 us (29%)
  other arithmetic  66.3 us (11%)
  matrix products  30.5 us (5%)
  starting transfers between devices  24.9 us (4%)
  between operations  19.7 us (3%)
    all_to_all x1, waiting for transfers between devices, per_device(): lax.all_to_all(grad_send.reshape(device_count, slot_count, BLOCK, 2, grou...  139 us
    ppermute x2, waiting for transfers between devices, padded_2(): lax.ppermute(lax.slice_in_dim(block, block.shape[dim] - width, None, axis...  75.9 us
    another operation x8, local copies, waits for them, and re-layouts, per_device(): jnp.stack((term_k, term_v), axis=2)  55.6 us
    psum x1, waiting for transfers between devices, broadcast(): return lax.psum(jnp.where(mine, array, jnp.zeros_like(array)), axis)  52.5 us
    reshape x4, local copies, waits for them, and re-layouts, assemble(): joined = joined.reshape(blocks, key_span, 2, GROUP_HEADS, HEAD_DIM)  43.8 us
    unnamed x66, local copies, waits for them, and re-layouts  19.5 us
    scatter-add x1, other arithmetic, per_device(): grad_owned = grad_owned.at[send_block, :, :, send_group, :].add(grad_back)  12.3 us
  transfers between devices with their start and end apart: 8, of which 3 were waited for; matrix products, arithmetic and copies ran while one was open for 17% of the time, Pallas kernels for 0%

profile of v1, /device:TPU:15, one launch (start us, length us, event | category | flops | bytes accessed | tf_op | source)
XLA Modules:
  0.0 578.7 jit_solution(12018558870932379248)
XLA Ops:
  12.2 2.8 gather_fusion
  15.0 4.5 broadcast_select_fusion
  19.4 6.7 %all-to-all-start = ((bf16[16,2,64,2,512]{4,2,3,1,0:T(8,128)(2,1)}), bf16[16,2,64,2,512]{4,2,3,1,0:T(8,128)(2,1)}, u32[]{:S(2)}, u32[]{:S(2)}) async-start(bf16[16,2,64,2,512]{4,2,3,1,0:T(8,128)(2,1)} %broadcast_select_fusion), calls=%async_computation | async-start | bytes 8388608 | tf_op jit(solution)/shard_map/all_to_all | solution.py:88
  32.5 3.4 collective-permute-start
  43.5 2.1 copy.245
  45.6 2.1 copy.244
  47.7 75.9 %collective-permute-done = bf16[1,64,2,1024]{3,1,2,0:T(8,128)(2,1)} collective-permute-done((bf16[1,64,2,1024]{3,1,2,0:T(8,128)(2,1)}, bf16[1,64,2,1024]{3,1,2,0:T(8,128)(2,1)}, u32[]{:S(2)}, u32[]{:S(2)}) %collective-permute-start) | collective-permute-done | bytes 262176 | tf_op jit(solution)/shard_map/ppermute | solution.py:19
  125.7 52.5 %all-reduce.5.cloned.1.call-done = (bf16[1,64,2,1024]{3,1,2,0:T(8,128)(2,1)}, bf16[1,64,2,1024]{3,1,2,0:T(8,128)(2,1)}) async-done(((bf16[1,64,2,1024]{3,1,2,0:T(8,128)(2,1)}, bf16[1,64,2,1024]{3,1,2,0:T(8,128)(2,1)}), (bf16[1,64,2,1024]{3,1,2,0:T(8,128)(2,1)}, bf16[1,64,2,1024]{3,1,2,0:T(8,128)(2,1)})) %all-reduce.5.cloned.1.call-update) | async-done | bytes 524304 | tf_op jit(solution)/shard_map/psum | solution.py:29
  184.9 2.9 gather_fusion.1
  189.7 10.0 %copy.239 = bf16[4,8,64,2,512]{2,1,4,0,3:T(8,128)(2,1)} copy(bf16[4,8,64,2,512]{4,2,3,1,0:T(8,128)(2,1)} %get-tuple-element.138) | data formatting | bytes 8388608 | tf_op jit(solution)/shard_map/reshape | solution.py:119
  199.7 11.8 %reshape.693 = bf16[4,512,2,8,64]{1,4,3,0,2:T(8,128)(2,1)} reshape(bf16[4,8,64,2,512]{2,1,4,0,3:T(8,128)(2,1)} %copy.239) | data formatting | bytes 8388608 | tf_op jit(solution)/shard_map/reshape | solution.py:119
  211.5 10.0 %copy.237 = bf16[4,8,64,2,512]{2,1,4,0,3:T(8,128)(2,1)} copy(bf16[4,8,64,2,512]{4,2,3,1,0:T(8,128)(2,1)} %get-tuple-element.137) | data formatting | bytes 8388608 | tf_op jit(solution)/shard_map/reshape | solution.py:119
  221.5 11.9 %reshape.692 = bf16[4,512,2,8,64]{1,4,3,0,2:T(8,128)(2,1)} reshape(bf16[4,8,64,2,512]{2,1,4,0,3:T(8,128)(2,1)} %copy.237) | data formatting | bytes 8388608 | tf_op jit(solution)/shard_map/reshape | solution.py:119
  233.5 2.4 fusion.25
  237.8 2.3 fusion.9
  240.2 2.2 multiply_reduce_fusion
  242.4 3.2 convolution_bitcast_fusion
  245.6 2.2 multiply_reduce_fusion.1
  247.9 3.2 convolution_bitcast_fusion.1
  251.1 2.2 fusion
  253.3 2.7 fusion.1
  256.0 7.1 %reshape.690 = f32[4,8,64,1,512]{2,1,4,0,3:T(8,128)} reshape(f32[4,512,8,64]{1,3,2,0:T(8,128)} %convolution_bitcast_fusion) | data formatting | bytes 8388608 | tf_op jit(solution)/shard_map/stack | solution.py:186
  263.1 6.8 %copy.235 = f32[4,8,64,1,512]{4,2,1,0,3:T(8,128)} copy(f32[4,8,64,1,512]{2,1,4,0,3:T(8,128)} %reshape.690) | data formatting | bytes 8388608 | tf_op jit(solution)/shard_map/stack | solution.py:186
  269.9 2.7 multiply_bitcast_fusion
  272.6 7.1 %reshape.689 = f32[4,8,64,1,512]{2,1,4,0,3:T(8,128)} reshape(f32[4,512,8,64]{1,3,2,0:T(8,128)} %multiply_bitcast_fusion) | data formatting | bytes 8388608 | tf_op jit(solution)/shard_map/stack | solution.py:186
  279.7 6.8 %copy.234 = f32[4,8,64,1,512]{4,2,1,0,3:T(8,128)} copy(f32[4,8,64,1,512]{2,1,4,0,3:T(8,128)} %reshape.689) | data formatting | bytes 8388608 | tf_op jit(solution)/shard_map/stack | solution.py:186
  286.5 7.1 %reshape.688 = f32[4,8,64,1,512]{2,1,4,0,3:T(8,128)} reshape(f32[4,512,8,64]{1,3,2,0:T(8,128)} %convolution_bitcast_fusion.1) | data formatting | bytes 8388608 | tf_op jit(solution)/shard_map/stack | solution.py:186
  293.5 7.0 %copy.233 = f32[4,8,64,1,512]{4,2,1,0,3:T(8,128)} copy(f32[4,8,64,1,512]{2,1,4,0,3:T(8,128)} %reshape.688) | data formatting | bytes 8388608 | tf_op jit(solution)/shard_map/stack | solution.py:186
  300.5 2.8 multiply_bitcast_fusion.1
  303.3 7.1 %reshape.687 = f32[4,8,64,1,512]{2,1,4,0,3:T(8,128)} reshape(f32[4,512,8,64]{1,3,2,0:T(8,128)} %multiply_bitcast_fusion.1) | data formatting | bytes 8388608 | tf_op jit(solution)/shard_map/stack | solution.py:186
  310.4 6.8 %copy.232 = f32[4,8,64,1,512]{4,2,1,0,3:T(8,128)} copy(f32[4,8,64,1,512]{2,1,4,0,3:T(8,128)} %reshape.687) | data formatting | bytes 8388608 | tf_op jit(solution)/shard_map/stack | solution.py:186
  322.7 2.3 fusion.27
  327.9 2.4 broadcast_in_dim.190
  330.3 7.8 %scatter_fusion = bf16[32,64,2,512]{3,1,2,0:T(8,128)(2,1)} fusion(bf16[32,64,2,512]{3,1,2,0:T(8,128)(2,1)} %broadcast_in_dim.190, s32[24]{0:T(128)S(1)} %fusion.86, bf16[24,64,2,512]{3,1,2,0:T(8,128)(2,1)S(1)} %bitcast.298), kind=kCustom, calls=%fused_computation.2 | custom fusion | bytes 9437280 | tf_op jit(solution)/shard_map/scatter | solution.py:203
  338.1 7.4 %all-to-all-start.1 = ((bf16[16,2,64,2,512]{4,2,3,1,0:T(8,128)(2,1)}), bf16[16,2,64,2,512]{4,2,3,1,0:T(8,128)(2,1)}, u32[]{:S(2)}, u32[]{:S(2)}) async-start(bf16[16,2,64,2,512]{4,2,3,1,0:T(8,128)(2,1)} %bitcast.287), calls=%async_computation.1 | async-start | bytes 8388608 | tf_op jit(solution)/shard_map/all_to_all | solution.py:205
  352.0 3.1 fusion.36
  355.4 2.3 fusion.37
  368.4 3.1 add_select_fusion
  371.5 5.6 scatter-add.45
  382.5 3.4 collective-permute-start.2
  387.7 139.0 %all-to-all-done.1 = bf16[16,2,64,2,512]{4,2,3,1,0:T(8,128)(2,1)} async-done(((bf16[16,2,64,2,512]{4,2,3,1,0:T(8,128)(2,1)}), bf16[16,2,64,2,512]{4,2,3,1,0:T(8,128)(2,1)}, u32[]{:S(2)}, u32[]{:S(2)}) %all-to-all-start.1) | async-done | bytes 4194336 | tf_op jit(solution)/shard_map/all_to_all | solution.py:205
  526.7 6.8 %convert_select_fusion = f32[32,64,2,512]{3,1,2,0:T(8,128)} fusion(bf16[16,2,64,2,512]{4,2,3,1,0:T(8,128)(2,1)} %all-to-all-done.1, pred[32]{0:T(512)(128)(4,1)S(1)} %gt.20), kind=kLoop, calls=%fused_computation.20 | loop fusion | flops 4194304 | bytes 12582944 | tf_op jit(solution)/shard_map/jit(_where)/select_n | solution.py:215
  533.8 12.3 %scatter_fusion.1 = f32[4,64,2,2,512]{4,1,3,2,0:T(8,128)S(1)} fusion(f32[4,64,2,2,512]{4,1,3,2,0:T(8,128)S(1)} %broadcast_in_dim.188, s32[32]{0:T(128)S(1)} %get-tuple-element.133, f32[32,64,2,512]{3,1,2,0:T(8,128)} %convert_select_fusion), kind=kCustom, calls=%fused_computation.3 | custom fusion | flops 2097152 | bytes 25166080 | tf_op jit(solution)/shard_map/scatter-add | solution.py:217
  546.1 2.9 copy.236
  549.1 4.2 reshape.691
  553.2 3.3 slice_add_fusion
  558.6 2.1 fusion.62
  560.7 7.8 %reduce_sum.109 = f32[2,64,2,1024]{3,1,2,0:T(8,128)S(1)} reduce(f32[16,2,64,2,1024]{4,2,3,1,0:T(8,128)} %all-gather.2.cloned.1.call-done, f32[]{:T(128)} %constant.389.clone.1), dimensions={0}, to_apply=%region_18.19 | reduce | flops 3932160 | bytes 17825796 | tf_op jit(solution)/shard_map/reduce_sum | solution.py:221
  (153 shorter events, 65.0 us)
Async XLA Ops:
  7.2 3.1 copy-start.26
  7.2 4.0 copy-start.27
  19.4 6.7 %copy-start.28 = (s32[2]{0:T(128)S(1)}, s32[2]{0:T(128)}, u32[]{:S(2)}) copy-start(s32[2]{0:T(128)} %param.31) | copy-start | bytes 28
  19.4 12.1 %copy-start.12 = (bf16[256,1024]{1,0:T(8,128)(2,1)S(1)}, bf16[256,1024]{1,0:T(8,128)(2,1)}, u32[]{:S(2)}) copy-start(bf16[256,1024]{1,0:T(8,128)(2,1)} %param.28) | copy-start | bytes 1572868
  19.4 12.1 %copy-start.13 = (bf16[256,1024]{1,0:T(8,128)(2,1)S(1)}, bf16[256,1024]{1,0:T(8,128)(2,1)}, u32[]{:S(2)}) copy-start(bf16[256,1024]{1,0:T(8,128)(2,1)} %param.29) | copy-start | bytes 1572868
  19.4 18.7 %copy-start.23 = (bf16[256,1024]{1,0:T(8,128)(2,1)S(1)}, bf16[256,1024]{1,0:T(8,128)(2,1)}, u32[]{:S(2)}) copy-start(bf16[256,1024]{1,0:T(8,128)(2,1)} %param.30) | copy-start | bytes 1572868
  19.4 165.4 %all-to-all-start = ((bf16[16,2,64,2,512]{4,2,3,1,0:T(8,128)(2,1)}), bf16[16,2,64,2,512]{4,2,3,1,0:T(8,128)(2,1)}, u32[]{:S(2)}, u32[]{:S(2)}) async-start(bf16[16,2,64,2,512]{4,2,3,1,0:T(8,128)(2,1)} %broadcast_select_fusion), calls=%async_computation | async-start | bytes 8388608 | tf_op jit(solution)/shard_map/all_to_all | solution.py:88
  26.1 152.0 %all-reduce.5.cloned.1.call-start = ((), (), s32[]{:S(2)}) async-start(), calls=%async_computation.3 | async-start | bytes 1048576 | tf_op jit(solution)/shard_map/psum | solution.py:29
  32.5 91.1 %collective-permute-start = (bf16[1,64,2,1024]{3,1,2,0:T(8,128)(2,1)}, bf16[1,64,2,1024]{3,1,2,0:T(8,128)(2,1)}, u32[]{:S(2)}, u32[]{:S(2)}) collective-permute-start(bf16[1,64,2,1024]{3,1,2,0:T(8,128)(2,1)} %get-tuple-element.154), channel_id=1, source_target_pairs={{0,1},{1,2},{2,3},{3,4},{4,5},{5,6},{6,7},{7,8},{8,9},{9,10},{10,1... | collective-permute-start | bytes 786440 | tf_op jit(solution)/shard_map/ppermute | solution.py:19
  35.8 145.3 %collective-permute-start.1 = (bf16[1,64,2,1024]{3,1,2,0:T(8,128)(2,1)S(1)}, bf16[1,64,2,1024]{3,1,2,0:T(8,128)(2,1)}, u32[]{:S(2)}, u32[]{:S(2)}) collective-permute-start(bf16[1,64,2,1024]{3,1,2,0:T(8,128)(2,1)S(1)} %get-tuple-element.155), channel_id=1, source_target_pairs={{1,0},{2,1},{3,2},{4,3},{5,4},{6,5},{7,6},{8,7},{9,8},{10,9},{11,1... | collective-permute-start | bytes 786440 | tf_op jit(solution)/shard_map/ppermute | solution.py:22
  37.8 522.9 %all-gather.2.cloned.1.call-start = ((), (), s32[]{:S(2)}) async-start(), calls=%async_computation.2 | async-start | bytes 17825792 | tf_op jit(solution)/shard_map/all_gather | solution.py:220
  221.5 11.9 %copy-start.18 = (bf16[4,64,1,8,64]{4,3,2,1,0:T(8,128)(2,1)S(1)}, bf16[4,64,1,8,64]{4,3,2,1,0:T(8,128)(2,1)}, u32[]{:S(2)}) copy-start(bf16[4,64,1,8,64]{4,3,2,1,0:T(8,128)(2,1)} %get-tuple-element.150) | copy-start | bytes 786436
  233.4 2.8 copy-start.15
  233.4 2.9 copy-start.17
  237.8 2.4 copy-start.14
  237.8 2.4 copy-start.20
  242.4 3.2 copy-start.19
  253.3 16.6 %copy-start.21 = (bf16[4,8,64,512]{3,2,1,0:T(8,128)(2,1)}, bf16[4,8,64,512]{3,2,1,0:T(8,128)(2,1)S(1)}, u32[]{:S(2)}) copy-start(bf16[4,8,64,512]{3,2,1,0:T(8,128)(2,1)S(1)} %fusion) | copy-start | bytes 6291460
  293.5 7.0 %copy-start.22 = (bf16[4,8,64,512]{3,2,1,0:T(8,128)(2,1)S(1)}, bf16[4,8,64,512]{3,2,1,0:T(8,128)(2,1)}, u32[]{:S(2)}) copy-start(bf16[4,8,64,512]{3,2,1,0:T(8,128)(2,1)} %fusion.1) | copy-start | bytes 6291460
  317.2 2.8 copy-start
  317.2 4.1 copy-start.3
  322.7 3.1 copy-start.6
  322.7 4.4 copy-start.8
  338.1 9.2 %copy-start.29 = (s32[4]{0:T(128)S(1)}, s32[4]{0:T(128)}, u32[]{:S(2)}) copy-start(s32[4]{0:T(128)} %constant.392.clone.1) | copy-start | bytes 52
  338.1 11.2 %copy-start.24 = (bf16[4,8,64,64]{3,2,1,0:T(8,128)(2,1)S(1)}, bf16[4,8,64,64]{3,2,1,0:T(8,128)(2,1)}, u32[]{:S(2)}) copy-start(bf16[4,8,64,64]{3,2,1,0:T(8,128)(2,1)} %get-tuple-element.165) | copy-start | bytes 786436
  338.1 11.2 %copy-start.25 = (bf16[4,8,64,64]{3,2,1,0:T(8,128)(2,1)S(1)}, bf16[4,8,64,64]{3,2,1,0:T(8,128)(2,1)}, u32[]{:S(2)}) copy-start(bf16[4,8,64,64]{3,2,1,0:T(8,128)(2,1)} %get-tuple-element.167) | copy-start | bytes 786436
  338.1 188.6 %all-to-all-start.1 = ((bf16[16,2,64,2,512]{4,2,3,1,0:T(8,128)(2,1)}), bf16[16,2,64,2,512]{4,2,3,1,0:T(8,128)(2,1)}, u32[]{:S(2)}, u32[]{:S(2)}) async-start(bf16[16,2,64,2,512]{4,2,3,1,0:T(8,128)(2,1)} %bitcast.287), calls=%async_computation.1 | async-start | bytes 8388608 | tf_op jit(solution)/shard_map/all_to_all | solution.py:205
  352.0 3.4 copy-start.16
  360.5 2.5 copy-start.9
  362.0 2.6 copy-start.7
  364.9 2.2 copy-start.1
  364.9 3.5 copy-start.4
  377.2 2.5 copy-start.2
  377.2 3.8 copy-start.5
  381.3 152.3 %copy-start.10 = (f32[6,64,2,1024]{3,1,0,2:T(8,128)}, f32[6,64,2,1024]{3,1,0,2:T(8,128)S(1)}, u32[]{:S(2)}) copy-start(f32[6,64,2,1024]{3,1,0,2:T(8,128)S(1)} %fusion.48) | copy-start | bytes 9437188
  382.5 174.1 %collective-permute-start.2 = (f32[1,64,2,1024]{3,1,0,2:T(8,128)}, f32[1,64,2,1024]{3,1,0,2:T(8,128)}, u32[]{:S(2)}, u32[]{:S(2)}) collective-permute-start(f32[1,64,2,1024]{3,1,0,2:T(8,128)} %get-tuple-element.136), channel_id=1, source_target_pairs={{0,1},{1,2},{2,3},{3,4},{4,5},{5,6},{6,7},{7,8},{8,9},{9,10},{10,1... | collective-permute-start | bytes 1572872 | tf_op jit(solution)/shard_map/ppermute | solution.py:19
  385.8 172.8 %collective-permute-start.3 = (f32[1,64,2,1024]{3,1,0,2:T(8,128)}, f32[1,64,2,1024]{3,1,0,2:T(8,128)}, u32[]{:S(2)}, u32[]{:S(2)}) collective-permute-start(f32[1,64,2,1024]{3,1,0,2:T(8,128)} %get-tuple-element.135), channel_id=1, source_target_pairs={{1,0},{2,1},{3,2},{4,3},{5,4},{6,5},{7,6},{8,7},{9,8},{10,9},{11,1... | collective-permute-start | bytes 1572872 | tf_op jit(solution)/shard_map/ppermute | solution.py:22
  549.1 4.2 copy-start.11
Sparse Core Ops, SparseCore 0:
  37.9 140.1 all-reduce.4
  322.8 205.6 all-gather.1
